TPU v7x, 512 devices: a whole 4x8x8 slice. The times are simulated.
512 devices in a mesh: rep: 8 (over y), exp: 64 (over x, z, core).
Axes of the slice: x: 4, y: 8, z: 8, core: 2. Of those that a mesh axis runs over, the one named last changes fastest.
Arguments:
- tokens: bfloat16 [65536, 1024], P(('rep', 'exp')), may hold values from -6 to 6
- cotangent: bfloat16 [65536, 1024], P(('rep', 'exp')), may hold values from -6 to 6
- expert_ids: int32 [65536, 2], P(('rep', 'exp')), may hold values from 0 to 63, all different within a row; in each aligned block of 128 rows (0 to 127, 128 to 255, ...) at most 8 rows name the same one
- combine_weight: float32 [65536, 2], P(('rep', 'exp')), may hold values from 0.2 to 1
- gate_weight: bfloat16 [64, 1024, 768], P('exp', 'rep'), may hold values from -0.1875 to 0.1875
- up_weight: bfloat16 [64, 1024, 768], P('exp', 'rep'), may hold values from -0.1875 to 0.1875
- down_weight: bfloat16 [64, 768, 1024], P('exp', None, 'rep'), may hold values from -0.21875 to 0.21875
Outputs:
- mixed: bfloat16 [65536, 1024], P(('rep', 'exp'))
- token_grad: bfloat16 [65536, 1024], P(('rep', 'exp'))
- gate_grad: bfloat16 [64, 1024, 768], P('exp', 'rep')
- up_grad: bfloat16 [64, 1024, 768], P('exp', 'rep')
- down_grad: bfloat16 [64, 768, 1024], P('exp', None, 'rep')
Inputs may be any that keep to these rules, and one draw needn't show every extreme that they name: `expert_ids`: each token names 2 different experts. Among the 128 tokens of one aligned block of rows, no expert is named more than 8 times, and in some block an expert is named exactly 8 times.
All inputs are finite; a program needn't handle non-finite values.
Results may differ from a plain program's by a relative error of at most 0.014.
Values may be sent and summed in bfloat16 or wider, within the bound.
No kernel may reach another device: no remote copies, remote signals or barrier semaphores. Data moves between devices by JAX's collectives and lax.ppermute only.
A program may use at most 64 MiB of HBM per device.

v0:
```python
import jax
import jax.numpy as jnp
from jax import lax
from jax.sharding import PartitionSpec as P


def slot_rows(block_ids, expert_count, capacity):
    flat = block_ids.reshape(-1)
    onehot = (flat[:, None] == jnp.arange(expert_count, dtype=jnp.int32)[None, :]).astype(jnp.int32)
    before = jnp.cumsum(onehot, axis=0) - onehot
    return flat * capacity + jnp.sum(before * onehot, axis=1)


def expert_forward(block_x, w_gate, w_up, w_down):
    gate_value = jnp.dot(block_x, w_gate, preferred_element_type=jnp.float32)
    up_value = jnp.dot(block_x, w_up, preferred_element_type=jnp.float32)
    swish_value = jax.nn.silu(gate_value)
    hidden = (swish_value * up_value).astype(jnp.bfloat16)
    output = jnp.dot(hidden, w_down, preferred_element_type=jnp.float32).astype(jnp.bfloat16)
    return (gate_value, up_value, swish_value, hidden, output)


def average_rows(received, replicas):
    features, hidden_units = received.shape
    stacked = received.reshape(replicas, features // replicas, hidden_units).astype(jnp.float32)
    return (jnp.sum(stacked, axis=0) / replicas).astype(jnp.bfloat16)


def per_device(tokens, cotangent, expert_ids, combine_weight, gate_weight, up_weight, down_weight):
    tok_rows, features = tokens.shape
    top_count = expert_ids.shape[1]
    groups = lax.axis_size("exp")
    replicas = lax.axis_size("rep")
    capacity = 2 * tok_rows * top_count // groups
    pair_count = tok_rows * top_count
    destination = slot_rows(expert_ids, groups, capacity)
    x_pairs = jnp.repeat(tokens, top_count, axis=0)
    cot_pairs = (combine_weight[:, :, None] * cotangent[:, None, :].astype(jnp.float32)).astype(
        jnp.bfloat16
    )
    cot_pairs = cot_pairs.reshape(pair_count, features)
    send_rows = jnp.zeros((groups * capacity, features), jnp.bfloat16).at[destination].set(x_pairs)
    send_cot = jnp.zeros((groups * capacity, features), jnp.bfloat16).at[destination].set(cot_pairs)
    w_gate, w_up, w_down = (
        lax.all_gather(gate_weight[0], "rep", axis=0, tiled=True),
        lax.all_gather(up_weight[0], "rep", axis=0, tiled=True),
        lax.all_gather(down_weight[0], "rep", axis=1, tiled=True),
    )
    recv_rows, recv_cot = (
        lax.all_to_all(send_rows, "exp", split_axis=0, concat_axis=0, tiled=True),
        lax.all_to_all(send_cot, "exp", split_axis=0, concat_axis=0, tiled=True),
    )
    gate_value, up_value, swish_value, hidden, output = expert_forward(
        recv_rows, w_gate, w_up, w_down
    )
    grad_hidden = lax.dot_general(
        recv_cot, w_down, (((1,), (1,)), ((), ())), preferred_element_type=jnp.float32
    )
    sigma = jax.nn.sigmoid(gate_value)
    grad_gate = (grad_hidden * up_value * sigma * (1.0 + gate_value * (1.0 - sigma))).astype(
        jnp.bfloat16
    )
    grad_up = (grad_hidden * swish_value).astype(jnp.bfloat16)
    grad_rows = (
        lax.dot_general(
            grad_gate, w_gate, (((1,), (1,)), ((), ())), preferred_element_type=jnp.float32
        )
        + lax.dot_general(
            grad_up, w_up, (((1,), (1,)), ((), ())), preferred_element_type=jnp.float32
        )
    ).astype(jnp.bfloat16)
    back_out, back_grad = (
        lax.all_to_all(output, "exp", split_axis=0, concat_axis=0, tiled=True),
        lax.all_to_all(grad_rows, "exp", split_axis=0, concat_axis=0, tiled=True),
    )
    part_gate = lax.dot_general(
        recv_rows, grad_gate, (((0,), (0,)), ((), ())), preferred_element_type=jnp.float32
    ).astype(jnp.bfloat16)
    part_up = lax.dot_general(
        recv_rows, grad_up, (((0,), (0,)), ((), ())), preferred_element_type=jnp.float32
    ).astype(jnp.bfloat16)
    part_down = lax.dot_general(
        recv_cot, hidden, (((0,), (0,)), ((), ())), preferred_element_type=jnp.float32
    ).astype(jnp.bfloat16)
    red_gate, red_up, red_down = (
        lax.all_to_all(part_gate, "rep", split_axis=0, concat_axis=0, tiled=True),
        lax.all_to_all(part_up, "rep", split_axis=0, concat_axis=0, tiled=True),
        lax.all_to_all(part_down, "rep", split_axis=0, concat_axis=0, tiled=True),
    )
    gate_grad = average_rows(red_gate, replicas)[None]
    up_grad = average_rows(red_up, replicas)[None]
    down_grad = average_rows(red_down, replicas).T[None]
    out_pairs = back_out[destination].reshape(tok_rows, top_count, features).astype(jnp.float32)
    mixed = jnp.sum(combine_weight[:, :, None] * out_pairs, axis=1).astype(jnp.bfloat16)
    grad_pairs = back_grad[destination].reshape(tok_rows, top_count, features).astype(jnp.float32)
    token_grad = jnp.sum(grad_pairs, axis=1).astype(jnp.bfloat16)
    return (mixed, token_grad, gate_grad, up_grad, down_grad)


def solution(mesh):
    placed = (
        P(("rep", "exp"), None),
        P(("rep", "exp"), None),
        P(("rep", "exp"), None),
        P(("rep", "exp"), None),
        P("exp", "rep", None),
        P("exp", "rep", None),
        P("exp", None, "rep"),
    )
    return jax.shard_map(
        per_device,
        mesh=mesh,
        in_specs=placed,
        out_specs=(
            P(("rep", "exp"), None),
            P(("rep", "exp"), None),
            P("exp", "rep", None),
            P("exp", "rep", None),
            P("exp", None, "rep"),
        ),
        check_vma=False,
    )
```

profile of v0, /device:TPU:1, one launch (start us, length us, event | category | flops | bytes accessed | tf_op | source)
XLA Modules:
  0.0 371.4 jit_solution(11726433471744356704)
XLA Ops:
  7.2 0.0 all-gather.9.cloned.1.call-start
  7.2 0.7 all-gather.9.cloned.1.call-update
  7.9 0.0 all-gather.7.cloned.1.call-start
  7.9 0.7 all-gather.7.cloned.1.call-update
  8.6 0.8 copy.15
  9.4 0.1 eq.29
  9.6 0.1 eq.25
  9.7 0.6 reduce-window.6
  10.3 0.2 slice_reduce_fusion
  10.6 0.7 broadcast_multiply_fusion
  11.3 0.1 copy.14
  11.4 0.1 mul.70
  11.5 1.2 broadcast_in_dim.4
  12.8 0.2 reshape.141
  13.0 0.1 fusion.37
  13.1 0.0 copy-start.3
  13.1 0.0 copy-start.2
  13.1 2.7 scatter_custom_fusion
  15.8 14.8 %all-to-all-start = ((bf16[64,8,1024]{2,1,0:T(8,128)(2,1)}), bf16[64,8,1024]{2,1,0:T(8,128)(2,1)S(1)}, u32[]{:S(2)}, u32[]{:S(2)}) async-start(bf16[64,8,1024]{2,1,0:T(8,128)(2,1)} %bitcast.3), calls=%async_computation | async-start | bytes 2097152 | tf_op jit(solution)/shard_map/all_to_all | solution.py:50
  30.6 0.0 all-gather.11.cloned.1.call-start
  30.7 0.7 all-gather.11.cloned.1.call-update
  31.4 0.1 copy.13
  31.5 0.1 mul.75
  31.7 0.3 mul.77
  31.9 0.7 mul.78
  32.7 2.8 scatter_custom_fusion.1
  35.5 23.7 %all-to-all-done = bf16[64,8,1024]{2,1,0:T(8,128)(2,1)S(1)} async-done(((bf16[64,8,1024]{2,1,0:T(8,128)(2,1)}), bf16[64,8,1024]{2,1,0:T(8,128)(2,1)S(1)}, u32[]{:S(2)}, u32[]{:S(2)}) %all-to-all-start) | async-done | bytes 1048608 | tf_op jit(solution)/shard_map/all_to_all | solution.py:50
  59.2 6.2 %all-to-all-start.2 = ((bf16[64,8,1024]{2,1,0:T(8,128)(2,1)}), bf16[64,8,1024]{2,1,0:T(8,128)(2,1)S(1)}, u32[]{:S(2)}, u32[]{:S(2)}) async-start(bf16[64,8,1024]{2,1,0:T(8,128)(2,1)} %bitcast.10), calls=%async_computation.2 | async-start | bytes 2097152 | tf_op jit(solution)/shard_map/all_to_all | solution.py:51
  65.4 0.0 all-gather.9.cloned.1.call-done
  65.4 3.5 fusion.5
  69.0 28.5 %all-gather.7.cloned.1.call-done = bf16[1,1024,768]{2,1,0:T(8,128)(2,1)} async-done(((bf16[1,128,768]{2,1,0:T(8,128)(2,1)}), bf16[1,1024,768]{2,1,0:T(8,128)(2,1)}) %all-gather.7.cloned.1.call-update) | async-done | bytes 1572880 | tf_op jit(solution)/shard_map/all_gather | solution.py:45
  97.5 3.5 fusion.9
  101.0 43.9 %all-gather.11.cloned.1.call-done = bf16[1,768,1024]{2,1,0:T(8,128)(2,1)} async-done(((bf16[1,768,128]{2,1,0:T(8,128)(2,1)}), bf16[1,768,1024]{2,1,0:T(8,128)(2,1)}) %all-gather.11.cloned.1.call-update) | async-done | bytes 1572880 | tf_op jit(solution)/shard_map/all_gather | solution.py:47
  145.0 4.9 %multiply_convert_fusion = (bf16[512,768]{1,0:T(8,128)(2,1)S(1)}, bf16[512,768]{1,0:T(8,128)(2,1)S(1)}, bf16[512,768]{1,0:T(8,128)(2,1)}) fusion(f32[512,768]{1,0:T(8,128)} %fusion.9, f32[512,768]{1,0:T(8,128)} %fusion.5, bf16[1,768,1024]{2,1,0:T(8,128)(2,1)} %all-gather.11.cloned.1.call-done, bf16[64,8,1024]{2,1,0:T(8,128)(2,1)S(1)} %all-to-all-done.2), kind=kOutput, calls=%fused_computation.22 | convolution fusion | flops 811204608 | bytes 8126464 | tf_op jit(solution)/shard_map/dot_general | solution.py:56
  149.9 1.0 fusion.7
  150.9 0.1 copy-done.6
  151.0 0.8 copy-done.4
  151.9 2.0 fusion.18
  153.9 15.0 %all-to-all-start.3 = ((bf16[64,8,1024]{2,1,0:T(8,128)(2,1)}), bf16[64,8,1024]{2,1,0:T(8,128)(2,1)S(1)}, u32[]{:S(2)}, u32[]{:S(2)}) async-start(bf16[64,8,1024]{2,1,0:T(8,128)(2,1)} %fusion.18), calls=%async_computation.3 | async-start | bytes 2097152 | tf_op jit(solution)/shard_map/all_to_all | solution.py:74
  168.9 3.4 fusion.15
  172.2 25.2 %all-to-all-done.3 = bf16[64,8,1024]{2,1,0:T(8,128)(2,1)S(1)} async-done(((bf16[64,8,1024]{2,1,0:T(8,128)(2,1)}), bf16[64,8,1024]{2,1,0:T(8,128)(2,1)S(1)}, u32[]{:S(2)}, u32[]{:S(2)}) %all-to-all-start.3) | async-done | bytes 1048608 | tf_op jit(solution)/shard_map/all_to_all | solution.py:74
  197.4 6.2 %all-to-all-start.1 = ((bf16[64,8,1024]{2,1,0:T(8,128)(2,1)}), bf16[64,8,1024]{2,1,0:T(8,128)(2,1)S(1)}, u32[]{:S(2)}, u32[]{:S(2)}) async-start(bf16[64,8,1024]{2,1,0:T(8,128)(2,1)} %fusion.15), calls=%async_computation.1 | async-start | bytes 2097152 | tf_op jit(solution)/shard_map/all_to_all | solution.py:73
  203.6 3.3 convolution_convert_fusion.2
  206.9 25.2 %all-to-all-done.1 = bf16[64,8,1024]{2,1,0:T(8,128)(2,1)S(1)} async-done(((bf16[64,8,1024]{2,1,0:T(8,128)(2,1)}), bf16[64,8,1024]{2,1,0:T(8,128)(2,1)S(1)}, u32[]{:S(2)}, u32[]{:S(2)}) %all-to-all-start.1) | async-done | bytes 1048608 | tf_op jit(solution)/shard_map/all_to_all | solution.py:73
  232.2 4.3 %all-to-all-start.4 = ((bf16[8,128,768]{2,1,0:T(8,128)(2,1)}), bf16[8,128,768]{2,1,0:T(8,128)(2,1)}, u32[]{:S(2)}, u32[]{:S(2)}) async-start(bf16[8,128,768]{2,1,0:T(8,128)(2,1)} %bitcast.89), calls=%async_computation.4 | async-start | bytes 3145728 | tf_op jit(solution)/shard_map/all_to_all | solution.py:86
  236.4 3.3 convolution_convert_fusion.1
  239.8 37.2 %all-to-all-done.4 = bf16[8,128,768]{2,1,0:T(8,128)(2,1)} async-done(((bf16[8,128,768]{2,1,0:T(8,128)(2,1)}), bf16[8,128,768]{2,1,0:T(8,128)(2,1)}, u32[]{:S(2)}, u32[]{:S(2)}) %all-to-all-start.4) | async-done | bytes 1572896 | tf_op jit(solution)/shard_map/all_to_all | solution.py:86
  277.0 4.4 %all-to-all-start.5 = ((bf16[8,128,768]{2,1,0:T(8,128)(2,1)}), bf16[8,128,768]{2,1,0:T(8,128)(2,1)}, u32[]{:S(2)}, u32[]{:S(2)}) async-start(bf16[8,128,768]{2,1,0:T(8,128)(2,1)} %bitcast.88), calls=%async_computation.5 | async-start | bytes 3145728 | tf_op jit(solution)/shard_map/all_to_all | solution.py:87
  281.4 3.3 convolution_convert_fusion
  284.7 34.9 %all-to-all-done.5 = bf16[8,128,768]{2,1,0:T(8,128)(2,1)} async-done(((bf16[8,128,768]{2,1,0:T(8,128)(2,1)}), bf16[8,128,768]{2,1,0:T(8,128)(2,1)}, u32[]{:S(2)}, u32[]{:S(2)}) %all-to-all-start.5) | async-done | bytes 1572896 | tf_op jit(solution)/shard_map/all_to_all | solution.py:87
  319.7 4.5 %all-to-all-start.6 = ((bf16[8,128,768]{2,1,0:T(8,128)(2,1)}), bf16[8,128,768]{2,1,0:T(8,128)(2,1)}, u32[]{:S(2)}, u32[]{:S(2)}) async-start(bf16[8,128,768]{2,1,0:T(8,128)(2,1)} %bitcast.87), calls=%async_computation.6 | async-start | bytes 3145728 | tf_op jit(solution)/shard_map/all_to_all | solution.py:88
  324.2 1.2 gather_fusion.1
  325.4 0.2 reshape.119
  325.6 2.1 reduce_sum.62
  327.7 1.2 gather_fusion
  328.8 0.7 reshape.120
  329.5 2.1 multiply_reduce_fusion
  331.6 1.7 convert_reduce_fusion.2
  333.2 1.7 convert_reduce_fusion.1
  334.9 0.7 fusion.32
  335.6 0.7 fusion.33
  336.3 26.1 %all-to-all-done.6 = bf16[8,128,768]{2,1,0:T(8,128)(2,1)} async-done(((bf16[8,128,768]{2,1,0:T(8,128)(2,1)}), bf16[8,128,768]{2,1,0:T(8,128)(2,1)}, u32[]{:S(2)}, u32[]{:S(2)}) %all-to-all-start.6) | async-done | bytes 1572896 | tf_op jit(solution)/shard_map/all_to_all | solution.py:88
  362.4 1.7 convert_reduce_fusion
  364.1 0.8 copy.19
  (21 shorter events, 0.1 us)
Async XLA Ops:
  7.2 58.3 %all-gather.9.cloned.1.call-start = ((), (), s32[]{:S(2)}) async-start(), calls=%async_computation.8 | async-start | bytes 1769472 | tf_op jit(solution)/shard_map/all_gather | solution.py:46
  7.9 89.6 %all-gather.7.cloned.1.call-start = ((), (), s32[]{:S(2)}) async-start(), calls=%async_computation.7 | async-start | bytes 1769472 | tf_op jit(solution)/shard_map/all_gather | solution.py:45
  13.1 18.3 %copy-start.3 = (f32[128,2]{0,1:T(2,128)S(1)}, f32[128,2]{0,1:T(2,128)}, u32[]{:S(2)}) copy-start(f32[128,2]{0,1:T(2,128)} %param.10) | copy-start | bytes 3076
  13.1 18.6 %copy-start.2 = (bf16[128,1024]{1,0:T(8,128)(2,1)S(1)}, bf16[128,1024]{1,0:T(8,128)(2,1)}, u32[]{:S(2)}) copy-start(bf16[128,1024]{1,0:T(8,128)(2,1)} %param.8) | copy-start | bytes 786436
  15.8 43.4 %all-to-all-start = ((bf16[64,8,1024]{2,1,0:T(8,128)(2,1)}), bf16[64,8,1024]{2,1,0:T(8,128)(2,1)S(1)}, u32[]{:S(2)}, u32[]{:S(2)}) async-start(bf16[64,8,1024]{2,1,0:T(8,128)(2,1)} %bitcast.3), calls=%async_computation | async-start | bytes 2097152 | tf_op jit(solution)/shard_map/all_to_all | solution.py:50
  30.6 114.3 %all-gather.11.cloned.1.call-start = ((), (), s32[]{:S(2)}) async-start(), calls=%async_computation.9 | async-start | bytes 1769472 | tf_op jit(solution)/shard_map/all_gather | solution.py:47
  59.2 41.8 %all-to-all-start.2 = ((bf16[64,8,1024]{2,1,0:T(8,128)(2,1)}), bf16[64,8,1024]{2,1,0:T(8,128)(2,1)S(1)}, u32[]{:S(2)}, u32[]{:S(2)}) async-start(bf16[64,8,1024]{2,1,0:T(8,128)(2,1)} %bitcast.10), calls=%async_computation.2 | async-start | bytes 2097152 | tf_op jit(solution)/shard_map/all_to_all | solution.py:51
  101.0 48.9 %copy-start = (bf16[64,8,1024]{2,1,0:T(8,128)(2,1)}, bf16[64,8,1024]{2,1,0:T(8,128)(2,1)S(1)}, u32[]{:S(2)}) copy-start(bf16[64,8,1024]{2,1,0:T(8,128)(2,1)S(1)} %all-to-all-done.2) | copy-start | bytes 3145732
  145.0 4.9 %copy-start.5 = (bf16[1,1024,768]{2,1,0:T(8,128)(2,1)S(1)}, bf16[1,1024,768]{2,1,0:T(8,128)(2,1)}, u32[]{:S(2)}) copy-start(bf16[1,1024,768]{2,1,0:T(8,128)(2,1)} %all-gather.7.cloned.1.call-done) | copy-start | bytes 4718596
  149.9 1.0 copy-start.7
  149.9 1.1 copy-start.6
  149.9 2.0 copy-start.4
  153.9 15.0 %copy-start.8 = (bf16[512,768]{1,0:T(8,128)(2,1)S(1)}, bf16[512,768]{1,0:T(8,128)(2,1)}, u32[]{:S(2)}) copy-start(bf16[512,768]{1,0:T(8,128)(2,1)} %get-tuple-element.12) | copy-start | bytes 2359300
  153.9 43.5 %all-to-all-start.3 = ((bf16[64,8,1024]{2,1,0:T(8,128)(2,1)}), bf16[64,8,1024]{2,1,0:T(8,128)(2,1)S(1)}, u32[]{:S(2)}, u32[]{:S(2)}) async-start(bf16[64,8,1024]{2,1,0:T(8,128)(2,1)} %fusion.18), calls=%async_computation.3 | async-start | bytes 2097152 | tf_op jit(solution)/shard_map/all_to_all | solution.py:74
  197.4 34.8 %all-to-all-start.1 = ((bf16[64,8,1024]{2,1,0:T(8,128)(2,1)}), bf16[64,8,1024]{2,1,0:T(8,128)(2,1)S(1)}, u32[]{:S(2)}, u32[]{:S(2)}) async-start(bf16[64,8,1024]{2,1,0:T(8,128)(2,1)} %fusion.15), calls=%async_computation.1 | async-start | bytes 2097152 | tf_op jit(solution)/shard_map/all_to_all | solution.py:73
  232.2 44.8 %all-to-all-start.4 = ((bf16[8,128,768]{2,1,0:T(8,128)(2,1)}), bf16[8,128,768]{2,1,0:T(8,128)(2,1)}, u32[]{:S(2)}, u32[]{:S(2)}) async-start(bf16[8,128,768]{2,1,0:T(8,128)(2,1)} %bitcast.89), calls=%async_computation.4 | async-start | bytes 3145728 | tf_op jit(solution)/shard_map/all_to_all | solution.py:86
  277.0 4.5 %copy-start.1 = (bf16[64,8,1024]{2,1,0:T(8,128)(2,1)S(1)}, bf16[64,8,1024]{2,1,0:T(8,128)(2,1)}, u32[]{:S(2)}) copy-start(bf16[64,8,1024]{2,1,0:T(8,128)(2,1)} %copy-done) | copy-start | bytes 3145732
  277.0 42.7 %all-to-all-start.5 = ((bf16[8,128,768]{2,1,0:T(8,128)(2,1)}), bf16[8,128,768]{2,1,0:T(8,128)(2,1)}, u32[]{:S(2)}, u32[]{:S(2)}) async-start(bf16[8,128,768]{2,1,0:T(8,128)(2,1)} %bitcast.88), calls=%async_computation.5 | async-start | bytes 3145728 | tf_op jit(solution)/shard_map/all_to_all | solution.py:87
  319.7 42.7 %all-to-all-start.6 = ((bf16[8,128,768]{2,1,0:T(8,128)(2,1)}), bf16[8,128,768]{2,1,0:T(8,128)(2,1)}, u32[]{:S(2)}, u32[]{:S(2)}) async-start(bf16[8,128,768]{2,1,0:T(8,128)(2,1)} %bitcast.87), calls=%async_computation.6 | async-start | bytes 3145728 | tf_op jit(solution)/shard_map/all_to_all | solution.py:88
Sparse Core Ops, SparseCore 0:
  10.1 43.9 all-gather.8
  56.1 41.3 all-gather.6
  99.5 45.4 all-gather.10
where the time goes:
time: 372 us; the launch traced here: 371 us
  waiting for transfers between devices  247 us (66%)
  starting transfers between devices  55.5 us (15%)
  matrix products  28.3 us (8%)
  other arithmetic  14.8 us (4%)
  between operations  14 us (4%)
  local copies, waits for them, and re-layouts  11.9 us (3%)
    all_gather x1, waiting for transfers between devices, per_device(): lax.all_gather(down_weight[0], 'rep', axis=1, tiled=True)  43.9 us
    all_to_all x1, waiting for transfers between devices, per_device(): lax.all_to_all(part_gate, 'rep', split_axis=0, concat_axis=0, tiled=True)  37.2 us
    all_to_all x1, waiting for transfers between devices, per_device(): lax.all_to_all(part_up, 'rep', split_axis=0, concat_axis=0, tiled=True)  34.9 us
    all_gather x1, waiting for transfers between devices, per_device(): lax.all_gather(gate_weight[0], 'rep', axis=0, tiled=True)  28.5 us
    all_to_all x1, waiting for transfers between devices, per_device(): lax.all_to_all(part_down, 'rep', split_axis=0, concat_axis=0, tiled=True)  26.1 us
    all_to_all x1, waiting for transfers between devices, per_device(): lax.all_to_all(output, 'exp', split_axis=0, concat_axis=0, tiled=True)  25.2 us
    all_to_all x1, waiting for transfers between devices, per_device(): lax.all_to_all(grad_rows, 'exp', split_axis=0, concat_axis=0, tiled=True)  25.2 us
    all_to_all x1, waiting for transfers between devices, per_device(): lax.all_to_all(send_rows, 'exp', split_axis=0, concat_axis=0, tiled=True)  23.7 us
  transfers between devices with their start and end apart: 10, of which 8 were waited for; matrix products, arithmetic and copies ran while one was open for 12% of the time, Pallas kernels for 0%

commit v1 on v0

--- a/solution.py
+++ b/solution.py
@@ -2,6 +2,28 @@
 import jax.numpy as jnp
 from jax import lax
 from jax.sharding import PartitionSpec as P
+
+
+def in_order(parts, dim):
+    shape = list(parts.shape[1:])
+    shape[dim] *= parts.shape[0]
+    return jnp.moveaxis(parts, 0, dim).reshape(shape)
+
+
+def ring_gather(x, axis, dim):
+    size = lax.axis_size(axis)
+    pairs = [(i, (i + 1) % size) for i in range(size)]
+    back = [(b, a) for a, b in pairs]
+    lower, upper = ([], [])
+    for step in range(size - 1):
+        if step % 2 == 0:
+            lower.append(lax.ppermute(lower[-1] if lower else x, axis, pairs))
+        else:
+            upper.append(lax.ppermute(upper[-1] if upper else x, axis, back))
+    blocks = jnp.stack([*lower[::-1], x, *upper])
+    shift = lax.axis_index(axis) - len(lower)
+    blocks = blocks[(jnp.arange(size) - shift) % size]
+    return in_order(blocks, dim)
 
 
 def slot_rows(block_ids, expert_count, capacity):
@@ -44,7 +66,7 @@
     w_gate, w_up, w_down = (
         lax.all_gather(gate_weight[0], "rep", axis=0, tiled=True),
         lax.all_gather(up_weight[0], "rep", axis=0, tiled=True),
-        lax.all_gather(down_weight[0], "rep", axis=1, tiled=True),
+        ring_gather(down_weight[0], "rep", 1),
     )
     recv_rows, recv_cot = (
         lax.all_to_all(send_rows, "exp", split_axis=0, concat_axis=0, tiled=True),

time: 372 us -> 341 us (0.917)
  waiting for transfers between devices: 247 us -> 182 us
  starting transfers between devices: 55.5 us -> 81.7 us
  local copies, waits for them, and re-layouts: 11.9 us -> 17.3 us
    all_gather x1 -> x0, waiting for transfers between devices: 43.9 us -> none  [per_device(): lax.all_gather(down_weight[0], 'rep', axis=1, tiled=True)]
    all_gather x1, waiting for transfers between devices: 28.5 us -> 2.34 us  [per_device(): lax.all_gather(gate_weight[0], 'rep', axis=0, tiled=True)]
    all_to_all x1, waiting for transfers between devices: 23.7 us -> 0.01 us  [per_device(): lax.all_to_all(send_rows, 'exp', split_axis=0, concat_axis=0, tiled=True)]
    ppermute x0 -> x7, starting transfers between devices: none -> 23 us  [the longest x3 14 us: ring_gather(): upper.append(lax.ppermute(upper[-1] if upper else x, axis, back))]
    ppermute x0 -> x7, waiting for transfers between devices: none -> 18 us  [the longest x4 17 us: ring_gather(): lower.append(lax.ppermute(lower[-1] if lower else x, axis, pairs))]
    all_to_all x1, waiting for transfers between devices: 0.01 us -> 12.5 us  [per_device(): lax.all_to_all(send_cot, 'exp', split_axis=0, concat_axis=0, tiled=True)]
    all_to_all x1, starting transfers between devices: 15 us -> 6.32 us  [per_device(): lax.all_to_all(grad_rows, 'exp', split_axis=0, concat_axis=0, tiled=True)]
    all_to_all x1, starting transfers between devices: 6.2 us -> 14.3 us  [per_device(): lax.all_to_all(send_cot, 'exp', split_axis=0, concat_axis=0, tiled=True)]
  transfers between devices with their start and end apart: 10 -> 16, of which waited for: 8 -> 10; matrix products, arithmetic and copies ran while one was open for 12% -> 15% of each run, Pallas kernels for 0% -> 0%
where the time goes in v1:
time: 341 us; the launch traced here: 339 us
  waiting for transfers between devices  182 us (53%)
  starting transfers between devices  81.7 us (24%)
  matrix products  28.8 us (8%)
  local copies, waits for them, and re-layouts  17.3 us (5%)
  other arithmetic  14.8 us (4%)
  between operations  14.5 us (4%)
    all_to_all x1, waiting for transfers between devices, per_device(): lax.all_to_all(part_gate, 'rep', split_axis=0, concat_axis=0, tiled=True)  37.3 us
    all_to_all x1, waiting for transfers between devices, per_device(): lax.all_to_all(part_up, 'rep', split_axis=0, concat_axis=0, tiled=True)  34.8 us
    all_to_all x1, waiting for transfers between devices, per_device(): lax.all_to_all(part_down, 'rep', split_axis=0, concat_axis=0, tiled=True)  26.1 us
    all_to_all x1, waiting for transfers between devices, per_device(): lax.all_to_all(grad_rows, 'exp', split_axis=0, concat_axis=0, tiled=True)  25.4 us
    all_to_all x1, waiting for transfers between devices, per_device(): lax.all_to_all(output, 'exp', split_axis=0, concat_axis=0, tiled=True)  25.2 us
    ppermute x4, waiting for transfers between devices, ring_gather(): lower.append(lax.ppermute(lower[-1] if lower else x, axis, pairs))  17 us
    all_to_all x1, starting transfers between devices, per_device(): lax.all_to_all(send_rows, 'exp', split_axis=0, concat_axis=0, tiled=True)  14.8 us
    all_to_all x1, starting transfers between devices, per_device(): lax.all_to_all(send_cot, 'exp', split_axis=0, concat_axis=0, tiled=True)  14.3 us
  transfers between devices with their start and end apart: 16, of which 10 were waited for; matrix products, arithmetic and copies ran while one was open for 15% of the time, Pallas kernels for 0%

profile of v1, /device:TPU:1, one launch (start us, length us, event | category | flops | bytes accessed | tf_op | source)
XLA Modules:
  0.0 339.4 jit_solution(1662494196450764715)
XLA Ops:
  7.2 0.7 all-gather.7.cloned.1.call-update
  7.9 0.8 copy.22
  8.8 0.1 eq.27
  9.0 0.6 reduce-window.6
  9.6 0.2 slice_reduce_fusion
  9.8 0.7 broadcast_multiply_fusion
  10.8 1.2 broadcast_in_dim.4
  12.0 0.2 reshape.202
  12.4 2.7 scatter_custom_fusion
  15.0 14.8 %all-to-all-start = ((bf16[64,8,1024]{2,1,0:T(8,128)(2,1)}), bf16[64,8,1024]{2,1,0:T(8,128)(2,1)S(1)}, u32[]{:S(2)}, u32[]{:S(2)}) async-start(bf16[64,8,1024]{2,1,0:T(8,128)(2,1)} %bitcast.3), calls=%async_computation | async-start | bytes 2097152 | tf_op jit(solution)/shard_map/all_to_all | solution.py:72
  29.9 3.2 collective-permute-start
  33.2 10.6 %collective-permute-done = bf16[768,128]{1,0:T(8,128)(2,1)S(1)} collective-permute-done((bf16[768,128]{1,0:T(8,128)(2,1)S(1)}, bf16[768,128]{1,0:T(8,128)(2,1)S(1)}, u32[]{:S(2)}, u32[]{:S(2)}) %collective-permute-start) | collective-permute-done | bytes 196640 | tf_op jit(solution)/shard_map/ppermute | solution.py:20
  43.8 1.9 collective-permute-start.1
  45.7 4.6 %collective-permute-start.4 = (bf16[768,128]{1,0:T(8,128)(2,1)S(1)}, bf16[768,128]{1,0:T(8,128)(2,1)}, u32[]{:S(2)}, u32[]{:S(2)}) collective-permute-start(bf16[768,128]{1,0:T(8,128)(2,1)S(1)} %bitcast.104), channel_id=1, source_target_pairs={{64,0},{128,64},{192,128},{256,192},{320,256},{384,320},{448,384},... | collective-permute-start | bytes 589832 | tf_op jit(solution)/shard_map/ppermute | solution.py:22
  50.3 6.4 %collective-permute-done.1 = bf16[768,128]{1,0:T(8,128)(2,1)} collective-permute-done((bf16[768,128]{1,0:T(8,128)(2,1)S(1)}, bf16[768,128]{1,0:T(8,128)(2,1)}, u32[]{:S(2)}, u32[]{:S(2)}) %collective-permute-start.1) | collective-permute-done | bytes 196640 | tf_op jit(solution)/shard_map/ppermute | solution.py:20
  56.7 1.9 collective-permute-start.2
  58.9 0.3 mul.77
  59.2 0.7 mul.78
  59.9 2.7 scatter_custom_fusion.1
  62.6 4.6 %collective-permute-start.5 = (bf16[768,128]{1,0:T(8,128)(2,1)}, bf16[768,128]{1,0:T(8,128)(2,1)S(1)}, u32[]{:S(2)}, u32[]{:S(2)}) collective-permute-start(bf16[768,128]{1,0:T(8,128)(2,1)} %collective-permute-done.4), channel_id=1, source_target_pairs={{64,0},{128,64},{192,128},{256,192},{320,256},{384,320},{448,384},... | collective-permute-start | bytes 589832 | tf_op jit(solution)/shard_map/ppermute | solution.py:22
  67.2 1.9 collective-permute-start.3
  69.2 0.9 collective-permute-done.5
  70.1 4.9 %collective-permute-start.6 = (bf16[768,128]{1,0:T(8,128)(2,1)S(1)}, bf16[768,128]{1,0:T(8,128)(2,1)}, u32[]{:S(2)}, u32[]{:S(2)}) collective-permute-start(bf16[768,128]{1,0:T(8,128)(2,1)S(1)} %collective-permute-done.5), channel_id=1, source_target_pairs={{64,0},{128,64},{192,128},{256,192},{320,256},{384,320},{448,384},... | collective-permute-start | bytes 589832 | tf_op jit(solution)/shard_map/ppermute | solution.py:22
  75.1 14.3 %all-to-all-start.2 = ((bf16[64,8,1024]{2,1,0:T(8,128)(2,1)}), bf16[64,8,1024]{2,1,0:T(8,128)(2,1)}, u32[]{:S(2)}, u32[]{:S(2)}) async-start(bf16[64,8,1024]{2,1,0:T(8,128)(2,1)} %bitcast.20), calls=%async_computation.2 | async-start | bytes 2097152 | tf_op jit(solution)/shard_map/all_to_all | solution.py:73
  89.4 1.0 bitcast_dynamic-update-slice_fusion.5
  90.4 1.0 bitcast_dynamic-update-slice_fusion.4
  91.4 1.0 bitcast_dynamic-update-slice_fusion.2
  92.4 1.0 bitcast_dynamic-update-slice_fusion
  93.4 0.9 gather_fusion
  94.2 0.7 copy.25
  95.0 4.5 %fusion.1 = f32[512,768]{1,0:T(8,128)} fusion(bf16[1,1024,768]{2,1,0:T(8,128)(2,1)} %all-gather.7.cloned.1.call-done, bf16[64,8,1024]{2,1,0:T(8,128)(2,1)} %copy-done.2), kind=kOutput, calls=%fused_computation.13 | convolution fusion | flops 805306368 | bytes 4194304 | tf_op jit(solution)/shard_map/dot_general | solution.py:38
  99.5 2.3 all-gather.5.cloned.1.call-done
  101.8 3.5 %fusion.5 = f32[512,768]{1,0:T(8,128)} fusion(bf16[1,1024,768]{2,1,0:T(8,128)(2,1)} %all-gather.5.cloned.1.call-done, bf16[64,8,1024]{2,1,0:T(8,128)(2,1)S(1)} %copy-done.3), kind=kOutput, calls=%fused_computation.17 | convolution fusion | flops 805306368 | bytes 4194304 | tf_op jit(solution)/shard_map/dot_general | solution.py:37
  105.4 12.5 %all-to-all-done.2 = bf16[64,8,1024]{2,1,0:T(8,128)(2,1)} async-done(((bf16[64,8,1024]{2,1,0:T(8,128)(2,1)}), bf16[64,8,1024]{2,1,0:T(8,128)(2,1)}, u32[]{:S(2)}, u32[]{:S(2)}) %all-to-all-start.2) | async-done | bytes 1048608 | tf_op jit(solution)/shard_map/all_to_all | solution.py:73
  117.9 4.6 %multiply_convert_fusion = (bf16[512,768]{1,0:T(8,128)(2,1)S(1)}, bf16[512,768]{1,0:T(8,128)(2,1)S(1)}, bf16[512,768]{1,0:T(8,128)(2,1)}) fusion(f32[512,768]{1,0:T(8,128)} %fusion.5, f32[512,768]{1,0:T(8,128)} %fusion.1, bf16[768,1024]{0,1:T(8,128)(2,1)S(1)} %bitcast.99, bf16[64,8,1024]{2,1,0:T(8,128)(2,1)} %all-to-all-done.2), kind=kOutput, calls=%fused_computation.19 | convolution fusion | flops 811204608 | bytes 8126464 | tf_op jit(solution)/shard_map/dot_general | solution.py:78
  122.5 1.0 fusion.3
  123.6 0.8 copy-done.10
  124.5 2.0 fusion.9
  126.5 6.3 %all-to-all-start.3 = ((bf16[64,8,1024]{2,1,0:T(8,128)(2,1)}), bf16[64,8,1024]{2,1,0:T(8,128)(2,1)S(1)}, u32[]{:S(2)}, u32[]{:S(2)}) async-start(bf16[64,8,1024]{2,1,0:T(8,128)(2,1)} %fusion.9), calls=%async_computation.3 | async-start | bytes 2097152 | tf_op jit(solution)/shard_map/all_to_all | solution.py:96
  132.8 3.1 fusion.8
  135.9 25.4 %all-to-all-done.3 = bf16[64,8,1024]{2,1,0:T(8,128)(2,1)S(1)} async-done(((bf16[64,8,1024]{2,1,0:T(8,128)(2,1)}), bf16[64,8,1024]{2,1,0:T(8,128)(2,1)S(1)}, u32[]{:S(2)}, u32[]{:S(2)}) %all-to-all-start.3) | async-done | bytes 1048608 | tf_op jit(solution)/shard_map/all_to_all | solution.py:96
  161.4 6.2 %all-to-all-start.1 = ((bf16[64,8,1024]{2,1,0:T(8,128)(2,1)}), bf16[64,8,1024]{2,1,0:T(8,128)(2,1)S(1)}, u32[]{:S(2)}, u32[]{:S(2)}) async-start(bf16[64,8,1024]{2,1,0:T(8,128)(2,1)} %fusion.8), calls=%async_computation.1 | async-start | bytes 2097152 | tf_op jit(solution)/shard_map/all_to_all | solution.py:95
  167.6 3.3 convolution_convert_fusion.2
  170.9 25.2 %all-to-all-done.1 = bf16[64,8,1024]{2,1,0:T(8,128)(2,1)S(1)} async-done(((bf16[64,8,1024]{2,1,0:T(8,128)(2,1)}), bf16[64,8,1024]{2,1,0:T(8,128)(2,1)S(1)}, u32[]{:S(2)}, u32[]{:S(2)}) %all-to-all-start.1) | async-done | bytes 1048608 | tf_op jit(solution)/shard_map/all_to_all | solution.py:95
  196.1 8.0 %all-to-all-start.4 = ((bf16[8,128,768]{2,1,0:T(8,128)(2,1)}), bf16[8,128,768]{2,1,0:T(8,128)(2,1)}, u32[]{:S(2)}, u32[]{:S(2)}) async-start(bf16[8,128,768]{2,1,0:T(8,128)(2,1)} %bitcast.102), calls=%async_computation.4 | async-start | bytes 3145728 | tf_op jit(solution)/shard_map/all_to_all | solution.py:108
  204.1 3.3 convolution_convert_fusion.1
  207.4 37.3 %all-to-all-done.4 = bf16[8,128,768]{2,1,0:T(8,128)(2,1)} async-done(((bf16[8,128,768]{2,1,0:T(8,128)(2,1)}), bf16[8,128,768]{2,1,0:T(8,128)(2,1)}, u32[]{:S(2)}, u32[]{:S(2)}) %all-to-all-start.4) | async-done | bytes 1572896 | tf_op jit(solution)/shard_map/all_to_all | solution.py:108
  244.7 4.4 %all-to-all-start.5 = ((bf16[8,128,768]{2,1,0:T(8,128)(2,1)}), bf16[8,128,768]{2,1,0:T(8,128)(2,1)}, u32[]{:S(2)}, u32[]{:S(2)}) async-start(bf16[8,128,768]{2,1,0:T(8,128)(2,1)} %bitcast.101), calls=%async_computation.5 | async-start | bytes 3145728 | tf_op jit(solution)/shard_map/all_to_all | solution.py:109
  249.1 3.4 %convolution_convert_fusion = bf16[1024,768]{1,0:T(8,128)(2,1)} fusion(bf16[512,768]{1,0:T(8,128)(2,1)S(1)} %copy-done.14, bf16[64,8,1024]{2,1,0:T(8,128)(2,1)} %all-to-all-done.2), kind=kOutput, calls=%fused_computation.9 | convolution fusion | flops 806092800 | bytes 3407872 | tf_op jit(solution)/shard_map/dot_general | solution.py:104
  252.5 34.8 %all-to-all-done.5 = bf16[8,128,768]{2,1,0:T(8,128)(2,1)} async-done(((bf16[8,128,768]{2,1,0:T(8,128)(2,1)}), bf16[8,128,768]{2,1,0:T(8,128)(2,1)}, u32[]{:S(2)}, u32[]{:S(2)}) %all-to-all-start.5) | async-done | bytes 1572896 | tf_op jit(solution)/shard_map/all_to_all | solution.py:109
  287.4 4.5 %all-to-all-start.6 = ((bf16[8,128,768]{2,1,0:T(8,128)(2,1)}), bf16[8,128,768]{2,1,0:T(8,128)(2,1)}, u32[]{:S(2)}, u32[]{:S(2)}) async-start(bf16[8,128,768]{2,1,0:T(8,128)(2,1)} %bitcast.98), calls=%async_computation.6 | async-start | bytes 3145728 | tf_op jit(solution)/shard_map/all_to_all | solution.py:110
  291.9 1.2 gather_fusion.2
  293.1 0.2 reshape.172
  293.3 2.1 reduce_sum.62
  295.4 1.2 gather_fusion.1
  296.5 0.7 reshape.173
  297.2 2.1 multiply_reduce_fusion
  299.3 1.7 convert_reduce_fusion.2
  300.9 1.7 convert_reduce_fusion.1
  302.6 0.7 fusion.24
  303.3 0.7 fusion.25
  304.0 26.1 %all-to-all-done.6 = bf16[8,128,768]{2,1,0:T(8,128)(2,1)} async-done(((bf16[8,128,768]{2,1,0:T(8,128)(2,1)}), bf16[8,128,768]{2,1,0:T(8,128)(2,1)}, u32[]{:S(2)}, u32[]{:S(2)}) %all-to-all-start.6) | async-done | bytes 1572896 | tf_op jit(solution)/shard_map/all_to_all | solution.py:110
  330.1 1.7 convert_reduce_fusion
  331.8 0.8 copy.27
  (56 shorter events, 1.3 us)
Async XLA Ops:
  7.2 87.8 %all-gather.7.cloned.1.call-start = ((), (), s32[]{:S(2)}) async-start(), calls=%async_computation.8 | async-start | bytes 1769472 | tf_op jit(solution)/shard_map/all_gather | solution.py:68
  12.3 17.6 %copy-start.6 = (bf16[1,768,128]{2,1,0:T(8,128)(2,1)S(1)}, bf16[1,768,128]{2,1,0:T(8,128)(2,1)}, u32[]{:S(2)}) copy-start(bf16[1,768,128]{2,1,0:T(8,128)(2,1)} %param.13) | copy-start | bytes 589828
  12.3 46.3 %copy-start.9 = (f32[128,2]{0,1:T(2,128)S(1)}, f32[128,2]{0,1:T(2,128)}, u32[]{:S(2)}) copy-start(f32[128,2]{0,1:T(2,128)} %param.10) | copy-start | bytes 3076
  12.3 46.5 %copy-start.5 = (bf16[128,1024]{1,0:T(8,128)(2,1)S(1)}, bf16[128,1024]{1,0:T(8,128)(2,1)}, u32[]{:S(2)}) copy-start(bf16[128,1024]{1,0:T(8,128)(2,1)} %param.8) | copy-start | bytes 786436
  15.0 60.0 %all-to-all-start = ((bf16[64,8,1024]{2,1,0:T(8,128)(2,1)}), bf16[64,8,1024]{2,1,0:T(8,128)(2,1)S(1)}, u32[]{:S(2)}, u32[]{:S(2)}) async-start(bf16[64,8,1024]{2,1,0:T(8,128)(2,1)} %bitcast.3), calls=%async_computation | async-start | bytes 2097152 | tf_op jit(solution)/shard_map/all_to_all | solution.py:72
  29.9 71.9 %all-gather.5.cloned.1.call-start = ((), (), s32[]{:S(2)}) async-start(), calls=%async_computation.7 | async-start | bytes 1769472 | tf_op jit(solution)/shard_map/all_gather | solution.py:67
  29.9 13.9 %collective-permute-start = (bf16[768,128]{1,0:T(8,128)(2,1)S(1)}, bf16[768,128]{1,0:T(8,128)(2,1)S(1)}, u32[]{:S(2)}, u32[]{:S(2)}) collective-permute-start(bf16[768,128]{1,0:T(8,128)(2,1)S(1)} %bitcast.103), channel_id=1, source_target_pairs={{0,64},{64,128},{128,192},{192,256},{256,320},{320,384},{384,448},... | collective-permute-start | bytes 589832 | tf_op jit(solution)/shard_map/ppermute | solution.py:20
  43.8 15.1 %copy-start.7 = (bf16[768,128]{1,0:T(8,128)(2,1)}, bf16[768,128]{1,0:T(8,128)(2,1)S(1)}, u32[]{:S(2)}) copy-start(bf16[768,128]{1,0:T(8,128)(2,1)S(1)} %collective-permute-done) | copy-start | bytes 589828
  43.8 12.9 %collective-permute-start.1 = (bf16[768,128]{1,0:T(8,128)(2,1)S(1)}, bf16[768,128]{1,0:T(8,128)(2,1)}, u32[]{:S(2)}, u32[]{:S(2)}) collective-permute-start(bf16[768,128]{1,0:T(8,128)(2,1)S(1)} %collective-permute-done), channel_id=1, source_target_pairs={{0,64},{64,128},{128,192},{192,256},{256,320},{320,384},{384,448},... | collective-permute-start | bytes 589832 | tf_op jit(solution)/shard_map/ppermute | solution.py:20
  45.7 16.9 %collective-permute-start.4 = (bf16[768,128]{1,0:T(8,128)(2,1)S(1)}, bf16[768,128]{1,0:T(8,128)(2,1)}, u32[]{:S(2)}, u32[]{:S(2)}) collective-permute-start(bf16[768,128]{1,0:T(8,128)(2,1)S(1)} %bitcast.104), channel_id=1, source_target_pairs={{64,0},{128,64},{192,128},{256,192},{320,256},{384,320},{448,384},... | collective-permute-start | bytes 589832 | tf_op jit(solution)/shard_map/ppermute | solution.py:22
  56.7 10.5 %collective-permute-start.2 = (bf16[768,128]{1,0:T(8,128)(2,1)}, bf16[768,128]{1,0:T(8,128)(2,1)}, u32[]{:S(2)}, u32[]{:S(2)}) collective-permute-start(bf16[768,128]{1,0:T(8,128)(2,1)} %collective-permute-done.1), channel_id=1, source_target_pairs={{0,64},{64,128},{128,192},{192,256},{256,320},{320,384},{384,448},... | collective-permute-start | bytes 589832 | tf_op jit(solution)/shard_map/ppermute | solution.py:20
  62.6 7.5 %collective-permute-start.5 = (bf16[768,128]{1,0:T(8,128)(2,1)}, bf16[768,128]{1,0:T(8,128)(2,1)S(1)}, u32[]{:S(2)}, u32[]{:S(2)}) collective-permute-start(bf16[768,128]{1,0:T(8,128)(2,1)} %collective-permute-done.4), channel_id=1, source_target_pairs={{64,0},{128,64},{192,128},{256,192},{320,256},{384,320},{448,384},... | collective-permute-start | bytes 589832 | tf_op jit(solution)/shard_map/ppermute | solution.py:22
  67.2 7.8 %collective-permute-start.3 = (bf16[768,128]{1,0:T(8,128)(2,1)}, bf16[768,128]{1,0:T(8,128)(2,1)S(1)}, u32[]{:S(2)}, u32[]{:S(2)}) collective-permute-start(bf16[768,128]{1,0:T(8,128)(2,1)} %collective-permute-done.2), channel_id=1, source_target_pairs={{0,64},{64,128},{128,192},{192,256},{256,320},{320,384},{384,448},... | collective-permute-start | bytes 589832 | tf_op jit(solution)/shard_map/ppermute | solution.py:20
  69.2 22.2 %copy-start.8 = (bf16[768,128]{1,0:T(8,128)(2,1)S(1)}, bf16[768,128]{1,0:T(8,128)(2,1)}, u32[]{:S(2)}) copy-start(bf16[768,128]{1,0:T(8,128)(2,1)} %copy-done.7) | copy-start | bytes 589828
  70.1 22.3 %collective-permute-start.6 = (bf16[768,128]{1,0:T(8,128)(2,1)S(1)}, bf16[768,128]{1,0:T(8,128)(2,1)}, u32[]{:S(2)}, u32[]{:S(2)}) collective-permute-start(bf16[768,128]{1,0:T(8,128)(2,1)S(1)} %collective-permute-done.5), channel_id=1, source_target_pairs={{64,0},{128,64},{192,128},{256,192},{320,256},{384,320},{448,384},... | collective-permute-start | bytes 589832 | tf_op jit(solution)/shard_map/ppermute | solution.py:22
  75.1 16.3 %copy-start.2 = (bf16[64,8,1024]{2,1,0:T(8,128)(2,1)}, bf16[64,8,1024]{2,1,0:T(8,128)(2,1)S(1)}, u32[]{:S(2)}) copy-start(bf16[64,8,1024]{2,1,0:T(8,128)(2,1)S(1)} %all-to-all-done) | copy-start | bytes 3145732
  75.1 42.8 %all-to-all-start.2 = ((bf16[64,8,1024]{2,1,0:T(8,128)(2,1)}), bf16[64,8,1024]{2,1,0:T(8,128)(2,1)}, u32[]{:S(2)}, u32[]{:S(2)}) async-start(bf16[64,8,1024]{2,1,0:T(8,128)(2,1)} %bitcast.20), calls=%async_computation.2 | async-start | bytes 2097152 | tf_op jit(solution)/shard_map/all_to_all | solution.py:73
  95.0 22.9 %copy-start = (bf16[768,8,128]{0,2,1:T(8,128)(2,1)}, bf16[768,8,128]{0,2,1:T(8,128)(2,1)S(1)}, u32[]{:S(2)}) copy-start(bf16[768,8,128]{0,2,1:T(8,128)(2,1)S(1)} %copy.25) | copy-start | bytes 4718596
  95.0 6.8 %copy-start.3 = (bf16[64,8,1024]{2,1,0:T(8,128)(2,1)S(1)}, bf16[64,8,1024]{2,1,0:T(8,128)(2,1)}, u32[]{:S(2)}) copy-start(bf16[64,8,1024]{2,1,0:T(8,128)(2,1)} %copy-done.2) | copy-start | bytes 3145732
  117.9 4.6 %copy-start.11 = (bf16[1,1024,768]{2,1,0:T(8,128)(2,1)S(1)}, bf16[1,1024,768]{2,1,0:T(8,128)(2,1)}, u32[]{:S(2)}) copy-start(bf16[1,1024,768]{2,1,0:T(8,128)(2,1)} %all-gather.5.cloned.1.call-done) | copy-start | bytes 4718596
  122.5 1.0 copy-start.13
  122.5 1.2 copy-start.12
  122.5 2.0 copy-start.10
  126.5 6.3 %copy-start.1 = (bf16[768,8,128]{0,2,1:T(8,128)(2,1)S(1)}, bf16[768,8,128]{0,2,1:T(8,128)(2,1)}, u32[]{:S(2)}) copy-start(bf16[768,8,128]{0,2,1:T(8,128)(2,1)} %copy-done) | copy-start | bytes 4718596
  126.5 34.9 %all-to-all-start.3 = ((bf16[64,8,1024]{2,1,0:T(8,128)(2,1)}), bf16[64,8,1024]{2,1,0:T(8,128)(2,1)S(1)}, u32[]{:S(2)}, u32[]{:S(2)}) async-start(bf16[64,8,1024]{2,1,0:T(8,128)(2,1)} %fusion.9), calls=%async_computation.3 | async-start | bytes 2097152 | tf_op jit(solution)/shard_map/all_to_all | solution.py:96
  135.9 31.6 %copy-start.4 = (bf16[64,8,1024]{2,1,0:T(8,128)(2,1)S(1)}, bf16[64,8,1024]{2,1,0:T(8,128)(2,1)}, u32[]{:S(2)}) copy-start(bf16[64,8,1024]{2,1,0:T(8,128)(2,1)} %copy-done.2) | copy-start | bytes 3145732
  161.4 34.8 %all-to-all-start.1 = ((bf16[64,8,1024]{2,1,0:T(8,128)(2,1)}), bf16[64,8,1024]{2,1,0:T(8,128)(2,1)S(1)}, u32[]{:S(2)}, u32[]{:S(2)}) async-start(bf16[64,8,1024]{2,1,0:T(8,128)(2,1)} %fusion.8), calls=%async_computation.1 | async-start | bytes 2097152 | tf_op jit(solution)/shard_map/all_to_all | solution.py:95
  196.1 48.6 %all-to-all-start.4 = ((bf16[8,128,768]{2,1,0:T(8,128)(2,1)}), bf16[8,128,768]{2,1,0:T(8,128)(2,1)}, u32[]{:S(2)}, u32[]{:S(2)}) async-start(bf16[8,128,768]{2,1,0:T(8,128)(2,1)} %bitcast.102), calls=%async_computation.4 | async-start | bytes 3145728 | tf_op jit(solution)/shard_map/all_to_all | solution.py:108
  244.7 4.4 %copy-start.14 = (bf16[512,768]{1,0:T(8,128)(2,1)S(1)}, bf16[512,768]{1,0:T(8,128)(2,1)}, u32[]{:S(2)}) copy-start(bf16[512,768]{1,0:T(8,128)(2,1)} %get-tuple-element.17) | copy-start | bytes 2359300
  244.7 42.7 %all-to-all-start.5 = ((bf16[8,128,768]{2,1,0:T(8,128)(2,1)}), bf16[8,128,768]{2,1,0:T(8,128)(2,1)}, u32[]{:S(2)}, u32[]{:S(2)}) async-start(bf16[8,128,768]{2,1,0:T(8,128)(2,1)} %bitcast.101), calls=%async_computation.5 | async-start | bytes 3145728 | tf_op jit(solution)/shard_map/all_to_all | solution.py:109
  287.4 42.7 %all-to-all-start.6 = ((bf16[8,128,768]{2,1,0:T(8,128)(2,1)}), bf16[8,128,768]{2,1,0:T(8,128)(2,1)}, u32[]{:S(2)}, u32[]{:S(2)}) async-start(bf16[8,128,768]{2,1,0:T(8,128)(2,1)} %bitcast.98), calls=%async_computation.6 | async-start | bytes 3145728 | tf_op jit(solution)/shard_map/all_to_all | solution.py:110
Sparse Core Ops, SparseCore 0:
  10.1 48.6 all-gather.6
  60.9 40.8 all-gather.4
